TPU v7x, 32 devices: a whole 2x2x4 slice. The times are simulated.
32 devices in a mesh: ty: 8 (over z, y), tx: 4 (over x, core).
Axes of the slice: x: 2, y: 2, z: 4, core: 2. Of those that a mesh axis runs over, the one named last changes fastest.
Arguments:
- density: bfloat16 [8, 256, 1024], P(None, 'ty', 'tx'), may hold values from 0 to 2
- stem_weight: bfloat16 [256, 72], replicated, may hold values from -0.75 to 0.75
- down_weight: bfloat16 [4, 512, 256], replicated, may hold values from -0.1875 to 0.1875
- depth_kernel: float32 [512, 7, 7], replicated, may hold values from -0.875 to 0.875
- mix_weight: bfloat16 [512, 512], replicated, may hold values from -0.25 to 0.25
- up_weight: bfloat16 [4, 256, 512], replicated, may hold values from -0.25 to 0.25
- head_weight: bfloat16 [4, 256], replicated, may hold values from -0.375 to 0.375
- cotangent: bfloat16 [4, 256, 1024], P(None, 'ty', 'tx'), may hold values from -24 to 24
- send_blocks: int32 [32, 128], P(('ty', 'tx')), may hold values from 0 to 255
- cell_slot: int32 [65536], P(('ty', 'tx')), may hold values from 0 to 127
- cell_offset: int32 [65536], P(('ty', 'tx')), may hold values from 0 to 127
- cell_area: float32 [65536], P(('ty', 'tx')), may hold values from 0.5 to 4
Outputs:
- congestion: bfloat16 [4, 256, 1024], P(None, 'ty', 'tx')
- cell_grad: float32 [65536], P(('ty', 'tx'))
Inputs may be any that keep to these rules, and one draw needn't show every extreme that they name: `send_blocks`: a local bin block index of the sending device. `cell_slot`: slots read by a cell; a few sending devices are read by many cells.
All inputs are finite; a program needn't handle non-finite values.
Results may differ from a plain program's by a relative error of at most 0.014.
Values may be sent and summed in bfloat16 or wider, within the bound.
No kernel may reach another device: no remote copies, remote signals or barrier semaphores. Data moves between devices by JAX's collectives and lax.ppermute only.
A program may use at most 192 MiB of HBM per device.

v0:
```python
import jax
import jax.numpy as jnp
from jax import lax
from jax.sharding import PartitionSpec as P


def with_halo(shard, sides, width):
    for axis, dim in sides:
        size, length = (lax.axis_size(axis), shard.shape[dim])
        up = [(i, (i + 1) % size) for i in range(size - 1)]
        down = [(j, i) for i, j in up]
        last = lax.slice_in_dim(shard, length - width, length, axis=dim)
        first = lax.slice_in_dim(shard, 0, width, axis=dim)
        before = lax.ppermute(last, axis, up)
        after = lax.ppermute(first, axis, down)
        shard = jnp.concatenate([before, shard, after], axis=dim)
    return shard


def silu_slope(value):
    sigma = jax.nn.sigmoid(value)
    return sigma * (1.0 + value * (1.0 - sigma))


def column_order(breadth):
    half = breadth // 2
    target = jnp.arange(breadth, dtype=jnp.int32)
    source = jnp.where(target < half, 2 * target, 2 * (target - half) + 1)
    return (jnp.arange(breadth, dtype=jnp.int32)[:, None] == source[None, :]).astype(jnp.float32)


def reorder_half(values, order):
    return jnp.dot(values, order.astype(jnp.bfloat16), preferred_element_type=jnp.float32).astype(
        jnp.bfloat16
    )


def restore_full(values, order):
    return jnp.dot(values, order.T, precision=lax.Precision.HIGHEST)


def restore_half(values, order):
    return jnp.dot(values, order.T.astype(jnp.bfloat16), preferred_element_type=jnp.float32).astype(
        jnp.bfloat16
    )


def stem_conv(padded, stem_weight, order):
    height = padded.shape[1] - 2
    breadth = padded.shape[2] - 2
    patches = jnp.concatenate(
        [
            padded[:, row_tap : row_tap + height, col_tap : col_tap + breadth]
            for row_tap in range(3)
            for col_tap in range(3)
        ],
        axis=0,
    )
    patches = reorder_half(patches, order)
    result = jnp.dot(
        stem_weight, patches.reshape(patches.shape[0], -1), preferred_element_type=jnp.float32
    )
    return result.reshape(stem_weight.shape[0], height, breadth)


def stride_down(feature_map, weights, transposed):
    depth_in, height, breadth = feature_map.shape
    half = breadth // 2
    paired = feature_map.reshape(depth_in, height // 2, 2, breadth)
    total = None
    for corner in range(4):
        matrix = weights[corner].T if transposed else weights[corner]
        row_part = corner // 2
        col_part = corner % 2
        picked = paired[:, :, row_part, col_part * half : (col_part + 1) * half]
        term = jnp.dot(matrix, picked.reshape(depth_in, -1), preferred_element_type=jnp.float32)
        total = term if total is None else total + term
    return total.reshape(total.shape[0], height // 2, half)


def stride_up(feature_map, weights, transposed):
    depth_in, height, breadth = feature_map.shape
    flat = feature_map.reshape(depth_in, -1)
    parts = []
    for corner in range(4):
        matrix = weights[corner].T if transposed else weights[corner]
        term = jnp.dot(matrix, flat, preferred_element_type=jnp.float32)
        parts.append(term.reshape(term.shape[0], height, breadth))
    outputs = parts[0].shape[0]
    upper = jnp.concatenate([parts[0], parts[1]], axis=2)
    lower = jnp.concatenate([parts[2], parts[3]], axis=2)
    return jnp.stack([upper, lower], axis=2).reshape(outputs, 2 * height, 2 * breadth)


def depthwise(padded, kernel):
    height = padded.shape[1] - 6
    breadth = padded.shape[2] - 6
    total = jnp.zeros((padded.shape[0], height, breadth), jnp.float32)
    for row_tap in range(7):
        for col_tap in range(7):
            total = (
                total
                + kernel[:, row_tap, col_tap][:, None, None]
                * padded[:, row_tap : row_tap + height, col_tap : col_tap + breadth]
            )
    return total


def depth_block(feature_map, depth_kernel, flipped):
    kernel = depth_kernel[:, ::-1, ::-1] if flipped else depth_kernel
    spread = lax.all_to_all(
        lax.all_to_all(feature_map, "ty", split_axis=0, concat_axis=1, tiled=True),
        "tx",
        split_axis=0,
        concat_axis=2,
        tiled=True,
    )
    owned = spread.shape[0]
    own_kernel = lax.dynamic_slice_in_dim(kernel, lax.axis_index(("ty", "tx")) * owned, owned, 0)
    padded = jnp.pad(spread, ((0, 0), (3, 3), (3, 3)))
    result = (spread + depthwise(padded, own_kernel)).astype(jnp.bfloat16)
    returned = lax.all_to_all(
        lax.all_to_all(result[None], "ty", split_axis=2, concat_axis=0, tiled=True),
        "tx",
        split_axis=3,
        concat_axis=1,
        tiled=True,
    )
    return returned.reshape(feature_map.shape)


def local(
    density,
    stem_weight,
    down_weight,
    depth_kernel,
    mix_weight,
    up_weight,
    head_weight,
    cotangent,
    send_blocks,
    cell_slot,
    cell_offset,
    cell_area,
):
    order = column_order(density.shape[2])
    padded_density = with_halo(density, (("ty", 1), ("tx", 2)), 1)
    features_pre = stem_conv(padded_density, stem_weight, order)
    features = jax.nn.silu(features_pre).astype(jnp.bfloat16)
    coarse_pre = stride_down(features, down_weight, False)
    coarse = jax.nn.silu(coarse_pre).astype(jnp.bfloat16)
    mixed = depth_block(coarse, depth_kernel, False)
    channels, half_rows, half_cols = coarse.shape
    hidden_pre = jnp.dot(
        mix_weight, mixed.reshape(channels, -1), preferred_element_type=jnp.float32
    ).reshape(channels, half_rows, half_cols)
    hidden_map = jax.nn.silu(hidden_pre).astype(jnp.bfloat16)
    skipped_pre = stride_up(hidden_map, up_weight, False) + features
    skipped = jax.nn.silu(skipped_pre).astype(jnp.bfloat16)
    wide, tile_rows, tile_cols = skipped.shape
    dies = head_weight.shape[0]
    head_out = jnp.dot(
        head_weight, skipped.reshape(wide, -1), preferred_element_type=jnp.float32
    ).reshape(dies, tile_rows, tile_cols)
    congestion = restore_full(head_out, order).astype(jnp.bfloat16)
    sorted_cotangent = reorder_half(cotangent, order)
    head_back = jnp.dot(
        head_weight.T, sorted_cotangent.reshape(dies, -1), preferred_element_type=jnp.float32
    ).reshape(wide, tile_rows, tile_cols)
    grad_skip = (silu_slope(skipped_pre) * head_back).astype(jnp.bfloat16)
    grad_hidden = (silu_slope(hidden_pre) * stride_down(grad_skip, up_weight, True)).astype(
        jnp.bfloat16
    )
    grad_mixed = (
        jnp.dot(mix_weight.T, grad_hidden.reshape(channels, -1), preferred_element_type=jnp.float32)
        .reshape(channels, half_rows, half_cols)
        .astype(jnp.bfloat16)
    )
    coarse_back = depth_block(grad_mixed, depth_kernel, True)
    grad_coarse = (silu_slope(coarse_pre) * coarse_back).astype(jnp.bfloat16)
    grad_features = (
        silu_slope(features_pre) * (grad_skip + stride_up(grad_coarse, down_weight, True))
    ).astype(jnp.bfloat16)
    in_maps = stem_weight.shape[1] // 9
    tap_weight = stem_weight.reshape(wide, 9, in_maps)[:, :, 0::2].reshape(wide, 9 * dies)
    natural_grad = restore_half(grad_features, order)
    padded_grad = with_halo(natural_grad, (("ty", 1), ("tx", 2)), 1)
    taps = jnp.dot(tap_weight.T, padded_grad.reshape(wide, -1), preferred_element_type=jnp.float32)
    taps = taps.reshape(9, dies, tile_rows + 2, tile_cols + 2)
    grad_bins = jnp.zeros((dies, tile_rows, tile_cols), jnp.float32)
    for row_tap in range(3):
        for col_tap in range(3):
            grad_bins = (
                grad_bins
                + taps[3 * row_tap + col_tap][
                    :, 2 - row_tap : 2 - row_tap + tile_rows, 2 - col_tap : 2 - col_tap + tile_cols
                ]
            )
    blocks = grad_bins.reshape(-1, 128)
    outgoing = jnp.take(blocks, send_blocks[0], axis=0)
    received = lax.all_to_all(outgoing, ("ty", "tx"), split_axis=0, concat_axis=0, tiled=True)
    slot_count = received.shape[0]
    slot_hot = (cell_slot[:, None] == jnp.arange(slot_count, dtype=jnp.int32)[None, :]).astype(
        jnp.float32
    )
    block_rows = jnp.dot(slot_hot, received, precision=lax.Precision.HIGHEST)
    offset_hot = (cell_offset[:, None] == jnp.arange(128, dtype=jnp.int32)[None, :]).astype(
        jnp.float32
    )
    picked = jnp.sum(block_rows * offset_hot, axis=1)
    cell_grad = cell_area * picked
    return (congestion, cell_grad)


def solution(mesh):
    in_specs = (
        P(None, "ty", "tx"),
        P(),
        P(),
        P(),
        P(),
        P(),
        P(),
        P(None, "ty", "tx"),
        P(("ty", "tx"), None),
        P(("ty", "tx")),
        P(("ty", "tx")),
        P(("ty", "tx")),
    )
    out_specs = (P(None, "ty", "tx"), P(("ty", "tx")))
    return jax.shard_map(local, mesh=mesh, in_specs=in_specs, out_specs=out_specs, check_vma=False)
```

profile of v0, /device:TPU:0, one launch (start us, length us, event | category | flops | bytes accessed | tf_op | source)
XLA Modules:
  0.0 912.9 jit_solution(14820096703275055703)
XLA Ops:
  2.8 5.5 collective-permute-start
  12.1 3.0 collective-permute-start.2
  23.1 3.3 copy-done.2
  26.3 2.2 multiply_convert_fusion.4
  32.0 2.8 add_add_fusion
  34.8 5.4 copy.81
  40.3 3.3 multiply_convert_fusion.5
  43.5 56.9 %all_to_all.141 = bf16[512,16,128]{2,1,0:T(8,128)(2,1)S(1)} all-to-all(bf16[512,16,128]{2,1,0:T(8,128)(2,1)S(1)} %multiply_convert_fusion.5), channel_id=1, replica_groups=mesh['ty'=8,'tx'=4] {'ty'}, dimensions={0} | all-to-all | bytes 4194304 | tf_op jit(solution)/shard_map/all_to_all | solution.py:112
  102.4 3.8 all-to-all-start.1
  106.4 25.4 %all-to-all-done.1 = bf16[64,128,128]{2,1,0:T(8,128)(2,1)S(1)} async-done(((bf16[64,128,128]{2,1,0:T(8,128)(2,1)}), bf16[64,128,128]{2,1,0:T(8,128)(2,1)S(1)}, u32[]{:S(2)}, u32[]{:S(2)}) %all-to-all-start.1) | async-done | bytes 2097184 | tf_op jit(solution)/shard_map/all_to_all | solution.py:111
  131.8 2.6 copy.83
  134.4 108.1 %fusion.76 = bf16[1,16,128,512]{2,3,1,0:T(8,128)(2,1)S(1)} fusion(bf16[16,128,512]{1,2,0:T(8,128)(2,1)} %bitcast.514, f32[16]{0:T(128)S(1)} %get-tuple-element.128, f32[16]{0:T(128)S(1)} %get-tuple-element.81, f32[16]{0:T(128)S(1)} %get-tuple-element.82, f32[16]{0:T(128)S(1)} %get-tuple-element.83, f32[16]{0:T(128)S(1)} %get-tuple-element.84, ...), kind=kLoop, calls=%fused_computation.208 | loop fusion | flops 155189248 | bytes 4197440 | tf_op jit(solution)/shard_map/broadcast_in_dim | solution.py:123
  242.6 3.4 copy.84
  246.0 52.1 %all_to_all.142 = bf16[1,16,128,512]{3,1,0,2:T(8,128)(2,1)S(1)} all-to-all(bf16[1,16,128,512]{3,1,0,2:T(8,128)(2,1)} %copy.84), channel_id=1, replica_groups=mesh['ty'=8,'tx'=4] {'ty'}, dimensions={2} | all-to-all | bytes 4194304 | tf_op jit(solution)/shard_map/all_to_all | solution.py:123
  298.1 24.4 %copy.86 = bf16[8,16,16,512]{2,0,1,3:T(8,128)(2,1)} copy(bf16[8,16,16,512]{3,1,2,0:T(8,128)(2,1)S(1)} %bitcast.507) | data formatting | bytes 4194304 | tf_op jit(solution)/shard_map/all_to_all | solution.py:123
  322.6 20.3 %reshape.211 = bf16[4,2,131072]{2,1,0:T(2,128)(2,1)} reshape(bf16[512,16,8,16]{3,2,1,0:T(8,128)(2,1)} %bitcast.491) | data formatting | bytes 4194304
  342.9 3.9 all-to-all-start.3
  347.1 4.6 fusion.182
  351.7 20.8 %all-to-all-done.3 = bf16[4,2,131072]{2,1,0:T(2,128)(2,1)S(1)} async-done(((bf16[4,2,131072]{2,1,0:T(2,128)(2,1)}), bf16[4,2,131072]{2,1,0:T(2,128)(2,1)S(1)}, u32[]{:S(2)}, u32[]{:S(2)}) %all-to-all-start.3) | async-done | bytes 2097184 | tf_op jit(solution)/shard_map/all_to_all | solution.py:122
  372.4 13.5 %reshape.212 = bf16[512,16,8,16]{3,2,1,0:T(8,128)(2,1)} reshape(bf16[4,2,131072]{2,1,0:T(2,128)(2,1)S(1)} %all-to-all-done.3) | data formatting | bytes 4194304
  386.0 17.1 %copy.105 = bf16[8,16,16,4,128]{4,3,2,1,0:T(4,128)(2,1)S(1)} copy(bf16[8,16,16,4,128]{2,0,1,4,3:T(8,128)(2,1)} %bitcast.492) | data formatting | bytes 4194304 | tf_op jit(solution)/shard_map/all_to_all | solution.py:122
  403.6 4.0 fusion.60
  407.6 2.0 fusion.90
  409.6 2.0 fusion.94
  411.6 2.1 fusion.82
  413.7 2.1 fusion.86
  415.8 6.4 maximum_bitcast_fusion
  423.0 10.1 %multiply_convert_fusion = (bf16[256,16,2,256]{0,3,2,1:T(8,128)(2,1)S(1)}, f32[256,16,2,256]{0,3,2,1:T(8,128)}) fusion(f32[256,16,2,256]{0,3,2,1:T(8,128)} %bitcast.489, f32[256,16,1,256]{0,3,2,1:T(8,128)} %get-tuple-element.132, f32[256,16,1,256]{0,3,2,1:T(8,128)S(1)} %get-tuple-element.131, f32[256,16,2,256]{0,3,2,1:T(8,128)S(1)} %bitcast.488), kind=kLoop, calls=%fused_computation.111 | loop fusion | flops 35651584 | bytes 37748736 | tf_op jit(solution)/shard_map/convert_element_type | solution.py:170
  433.3 2.8 fusion.84
  436.1 2.7 fusion.92
  438.8 2.7 fusion.88
  441.5 8.2 convolution_convert_fusion
  449.7 3.4 copy.94
  453.1 51.3 %all_to_all.143 = bf16[512,16,128]{2,1,0:T(8,128)(2,1)S(1)} all-to-all(bf16[512,16,128]{2,1,0:T(8,128)(2,1)S(1)} %copy.94), channel_id=1, replica_groups=mesh['ty'=8,'tx'=4] {'ty'}, dimensions={0} | all-to-all | bytes 4194304 | tf_op jit(solution)/shard_map/all_to_all | solution.py:112
  506.4 4.0 all-to-all-start.5
  510.7 25.3 %all-to-all-done.5 = bf16[64,128,128]{2,1,0:T(8,128)(2,1)S(1)} async-done(((bf16[64,128,128]{2,1,0:T(8,128)(2,1)}), bf16[64,128,128]{2,1,0:T(8,128)(2,1)S(1)}, u32[]{:S(2)}, u32[]{:S(2)}) %all-to-all-start.5) | async-done | bytes 2097184 | tf_op jit(solution)/shard_map/all_to_all | solution.py:111
  536.0 2.6 copy.96
  538.6 106.8 %fusion.75 = bf16[1,16,128,512]{2,3,1,0:T(8,128)(2,1)S(1)} fusion(bf16[16,128,512]{1,2,0:T(8,128)(2,1)} %bitcast.515, f32[16]{0:T(128)S(1)} %get-tuple-element.79, f32[16]{0:T(128)S(1)} %get-tuple-element.32, f32[16]{0:T(128)S(1)} %get-tuple-element.33, f32[16]{0:T(128)S(1)} %get-tuple-element.34, f32[16]{0:T(128)S(1)} %get-tuple-element.35, ...), kind=kLoop, calls=%fused_computation.207 | loop fusion | flops 155189248 | bytes 4197440 | tf_op jit(solution)/shard_map/broadcast_in_dim | solution.py:123
  645.4 3.2 copy.97
  648.6 51.7 %all_to_all.144 = bf16[1,16,128,512]{3,1,0,2:T(8,128)(2,1)S(1)} all-to-all(bf16[1,16,128,512]{3,1,0,2:T(8,128)(2,1)} %copy.97), channel_id=1, replica_groups=mesh['ty'=8,'tx'=4] {'ty'}, dimensions={2} | all-to-all | bytes 4194304 | tf_op jit(solution)/shard_map/all_to_all | solution.py:123
  700.4 24.5 %copy.99 = bf16[8,16,16,512]{2,0,1,3:T(8,128)(2,1)} copy(bf16[8,16,16,512]{3,1,2,0:T(8,128)(2,1)S(1)} %bitcast.509) | data formatting | bytes 4194304 | tf_op jit(solution)/shard_map/all_to_all | solution.py:123
  724.8 20.3 %reshape.213 = bf16[4,2,131072]{2,1,0:T(2,128)(2,1)} reshape(bf16[512,16,8,16]{3,2,1,0:T(8,128)(2,1)} %bitcast.493) | data formatting | bytes 4194304
  745.2 3.6 all-to-all-start.7
  748.8 9.0 copy.93
  759.2 9.1 copy.89
  768.2 9.3 %copy.91 = f32[256,16,2,256]{3,0,2,1:T(8,128)} copy(f32[256,16,2,256]{0,3,2,1:T(8,128)} %get-tuple-element.3) | data formatting | bytes 16777216 | tf_op jit(solution)/shard_map/stack | solution.py:92
  777.5 13.5 %reshape.214 = bf16[512,16,8,16]{3,2,1,0:T(8,128)(2,1)} reshape(bf16[4,2,131072]{2,1,0:T(2,128)(2,1)S(1)} %all-to-all-done.7) | data formatting | bytes 4194304
  791.1 16.0 %copy.100 = bf16[8,16,16,512]{3,2,1,0:T(8,128)(2,1)S(1)} copy(bf16[8,16,16,512]{2,0,1,3:T(8,128)(2,1)} %bitcast.494) | data formatting | bytes 4194304 | tf_op jit(solution)/shard_map/all_to_all | solution.py:122
  807.1 3.0 reshape.190
  810.1 2.7 copy.101
  812.8 4.0 copy.123
  816.8 5.5 copy.102
  822.4 5.0 fusion.66
  830.9 3.8 pad_maximum_fusion.1
  834.7 9.3 %copy.103 = f32[256,16,2,256]{3,0,2,1:T(8,128)} copy(f32[256,16,2,256]{0,3,1,2:T(8,128)} %pad_maximum_fusion.1) | data formatting | bytes 16777216 | tf_op jit(solution)/shard_map/stack | solution.py:92
  844.0 13.6 %fusion.1 = bf16[256,32,256]{2,0,1:T(8,128)(2,1)S(1)} fusion(f32[256,16,2,256]{3,0,2,1:T(8,128)} %copy.103, f32[256,32,256]{2,0,1:T(8,128)} %copy.89, f32[256,32,256]{2,0,1:T(8,128)} %copy.93, f32[256,16,2,256]{3,0,2,1:T(8,128)} %copy.91), kind=kLoop, calls=%fused_computation.102 | loop fusion | flops 50331648 | bytes 37748736 | tf_op jit(solution)/shard_map/convert_element_type | solution.py:183
  860.2 4.6 collective-permute-start.4
  864.8 8.3 multiply_convert_fusion.3
  874.5 3.0 collective-permute-start.6
  878.8 3.9 pad_maximum_fusion.2
  882.6 7.6 reshape.185
  890.3 3.7 convolution_bitcast_fusion
  897.4 5.7 all-to-all-start.8
  904.1 6.5 all-to-all-done.8
  (116 shorter events, 39.2 us)
Async XLA Ops:
  0.6 402.9 %copy-start = (bf16[512,512]{1,0:T(8,128)(2,1)S(1)}, bf16[512,512]{1,0:T(8,128)(2,1)}, u32[]{:S(2)}) copy-start(bf16[512,512]{1,0:T(8,128)(2,1)} %param.16) | copy-start | bytes 1572868
  1.5 6.8 collective-permute-start.1
  2.8 6.9 collective-permute-start
  10.7 11.1 %copy-start.7 = (bf16[256,72]{0,1:T(8,128)(2,1)S(1)}, bf16[256,72]{0,1:T(8,128)(2,1)}, u32[]{:S(2)}) copy-start(bf16[256,72]{0,1:T(8,128)(2,1)} %param.13) | copy-start | bytes 110596
  10.8 4.4 collective-permute-start.3
  12.1 3.9 collective-permute-start.2
  15.1 331.7 %copy-start.8 = (s32[256]{0:T(256)}, s32[256]{0:T(256)S(1)}, u32[]{:S(2)}) copy-start(s32[256]{0:T(256)S(1)} %fusion.143) | copy-start | bytes 3076
  23.1 3.3 copy-start.2
  28.6 1.2 copy-start.3
  100.5 5.7 copy-start.6
  102.4 29.4 %all-to-all-start.1 = ((bf16[64,128,128]{2,1,0:T(8,128)(2,1)}), bf16[64,128,128]{2,1,0:T(8,128)(2,1)S(1)}, u32[]{:S(2)}, u32[]{:S(2)}) async-start(bf16[64,128,128]{2,1,0:T(8,128)(2,1)} %bitcast.511), calls=%async_computation.1 | async-start | bytes 4194304 | tf_op jit(solution)/shard_map/all_to_all | solution.py:111
  342.9 3.9 copy-start.13
  342.9 4.2 copy-start.10
  342.9 29.5 %all-to-all-start.3 = ((bf16[4,2,131072]{2,1,0:T(2,128)(2,1)}), bf16[4,2,131072]{2,1,0:T(2,128)(2,1)S(1)}, u32[]{:S(2)}, u32[]{:S(2)}) async-start(bf16[4,2,131072]{2,1,0:T(2,128)(2,1)} %reshape.211), calls=%async_computation.3 | async-start | bytes 4194304 | tf_op jit(solution)/shard_map/all_to_all | solution.py:122
  403.6 4.0 copy-start.5
  415.8 6.5 slice-start
  415.8 7.2 slice-start.1
  506.4 29.6 %all-to-all-start.5 = ((bf16[64,128,128]{2,1,0:T(8,128)(2,1)}), bf16[64,128,128]{2,1,0:T(8,128)(2,1)S(1)}, u32[]{:S(2)}, u32[]{:S(2)}) async-start(bf16[64,128,128]{2,1,0:T(8,128)(2,1)} %bitcast.513), calls=%async_computation.5 | async-start | bytes 4194304 | tf_op jit(solution)/shard_map/all_to_all | solution.py:111
  745.2 32.4 %all-to-all-start.7 = ((bf16[4,2,131072]{2,1,0:T(2,128)(2,1)}), bf16[4,2,131072]{2,1,0:T(2,128)(2,1)S(1)}, u32[]{:S(2)}, u32[]{:S(2)}) async-start(bf16[4,2,131072]{2,1,0:T(2,128)(2,1)} %reshape.213), calls=%async_computation.7 | async-start | bytes 4194304 | tf_op jit(solution)/shard_map/all_to_all | solution.py:122
  748.8 9.6 %copy-start.16 = (s32[1,128]{1,0:T(1,128)S(1)}, s32[1,128]{1,0:T(1,128)}, u32[]{:S(2)}) copy-start(s32[1,128]{1,0:T(1,128)} %param.20) | copy-start | bytes 1540
  822.4 5.0 copy-start.4
  844.0 13.6 %copy-start.9 = (s32[256]{0:T(256)S(1)}, s32[256]{0:T(256)}, u32[]{:S(2)}) copy-start(s32[256]{0:T(256)} %copy-done.8) | copy-start | bytes 3076
  858.9 14.2 %collective-permute-start.5 = (bf16[256,1,256]{0,2,1:T(8,128)(2,1)S(1)}, bf16[256,1,256]{0,2,1:T(8,128)(2,1)S(1)}, u32[]{:S(2)}, u32[]{:S(2)}) collective-permute-start(bf16[256,1,256]{0,2,1:T(8,128)(2,1)S(1)} %get-tuple-element.7), channel_id=1, source_target_pairs={{4,0},{8,4},{12,8},{16,12},{20,16},{24,20},{28,24},{5,1},{9,5},{13... | collective-permute-start | bytes 393224 | tf_op jit(solution)/shard_map/ppermute | solution.py:15
  860.2 12.9 %collective-permute-start.4 = (bf16[256,1,256]{0,2,1:T(8,128)(2,1)S(1)}, bf16[256,1,256]{0,2,1:T(8,128)(2,1)S(1)}, u32[]{:S(2)}, u32[]{:S(2)}) collective-permute-start(bf16[256,1,256]{0,2,1:T(8,128)(2,1)S(1)} %get-tuple-element.6), channel_id=1, source_target_pairs={{0,4},{4,8},{8,12},{12,16},{16,20},{20,24},{24,28},{1,5},{5,9},{9,... | collective-permute-start | bytes 393224 | tf_op jit(solution)/shard_map/ppermute | solution.py:14
  873.1 4.4 copy-start.11
  873.2 5.5 collective-permute-start.7
  874.5 4.2 collective-permute-start.6
  894.0 16.6 %copy-start.14 = (s32[2048]{0:T(1024)S(1)}, s32[2048]{0:T(1024)}, u32[]{:S(2)}) copy-start(s32[2048]{0:T(1024)} %param.21) | copy-start | bytes 24580
  894.0 16.6 %copy-start.15 = (s32[2048]{0:T(1024)S(1)}, s32[2048]{0:T(1024)}, u32[]{:S(2)}) copy-start(s32[2048]{0:T(1024)} %param.22) | copy-start | bytes 24580
  894.0 18.4 %copy-start.1 = (bf16[512,512]{1,0:T(8,128)(2,1)S(1)}, bf16[512,512]{1,0:T(8,128)(2,1)}, u32[]{:S(2)}) copy-start(bf16[512,512]{1,0:T(8,128)(2,1)} %param.16) | copy-start | bytes 1572868
  894.2 17.6 %copy-start.12 = (f32[2048]{0:T(1024)S(1)}, f32[2048]{0:T(1024)}, u32[]{:S(2)}) copy-start(f32[2048]{0:T(1024)} %param.23) | copy-start | bytes 24580
  897.4 13.1 %all-to-all-start.8 = ((f32[32,4,128]{2,1,0:T(4,128)}), f32[32,4,128]{2,1,0:T(4,128)S(1)}, u32[]{:S(2)}, u32[]{:S(2)}) async-start(f32[32,4,128]{2,1,0:T(4,128)} %broadcast_select_fusion), calls=%async_computation.8 | async-start | bytes 131072 | tf_op jit(solution)/shard_map/all_to_all | solution.py:201
where the time goes:
time: 923 us; the launch traced here: 913 us
  other arithmetic  279 us (30%)
  local copies, waits for them, and re-layouts  246 us (27%)
  blocking collectives  212 us (23%)
  waiting for transfers between devices  80.2 us (9%)
  matrix products  51.3 us (6%)
  starting transfers between devices  42.4 us (5%)
    broadcast_in_dim x2, other arithmetic, depth_block(): result[None]  215 us
    all_to_all x2, blocking collectives, depth_block(): lax.all_to_all(feature_map, 'ty', split_axis=0, concat_axis=1, tiled=True)  108 us
    all_to_all x2, blocking collectives, depth_block(): lax.all_to_all(result[None], 'ty', split_axis=2, concat_axis=0, tiled=True)  104 us
    unnamed x52, local copies, waits for them, and re-layouts  79.2 us
    all_to_all x2, waiting for transfers between devices, depth_block(): lax.all_to_all(lax.all_to_all(feature_map, 'ty', split_axis=0, concat_axi...  50.7 us
    all_to_all x2, local copies, waits for them, and re-layouts, depth_block(): lax.all_to_all(result[None], 'ty', split_axis=2, concat_axis=0, tiled=True)  48.9 us
    all_to_all x3, local copies, waits for them, and re-layouts, depth_block(): lax.all_to_all(lax.all_to_all(result[None], 'ty', split_axis=2, concat_ax...  33.6 us
    all_to_all x2, waiting for transfers between devices, depth_block(): lax.all_to_all(lax.all_to_all(result[None], 'ty', split_axis=2, concat_ax...  20.8 us
  transfers between devices with their start and end apart: 13, of which 6 were waited for; matrix products, arithmetic and copies ran while one was open for 5% of the time, Pallas kernels for 0%

commit v1 on v0

v1 whole, which is shorter than its diff:
```python
import functools

import jax
import jax.numpy as jnp
import numpy as np
from jax import lax
from jax.experimental import pallas as pl
from jax.experimental.pallas import tpu as pltpu
from jax.sharding import PartitionSpec as P


REACH = 7
MIDDLE = 4
EDGE = 1
MARGIN = 8
GUARD = 8
CHUNK = 3
ROW_ORDER = (1, 2, 3, 0)

NT = (((1,), (1,)), ((), ()))
f32 = jnp.float32
bf16 = jnp.bfloat16


def dot(a, b):
    return jnp.dot(a, b, preferred_element_type=f32)


def dot_nt(a, b):
    return lax.dot_general(a, b, NT, preferred_element_type=f32)


def sigmoid(value):
    return 0.5 * jnp.tanh(0.5 * value) + 0.5


def stem_selectors(maps, dies):
    table = np.zeros((4, 16 * maps + 16 * dies, 9 * maps), np.float32)
    for p in range(2):
        for q in range(2):
            tap = 2 * p + q
            for a in range(3):
                for b in range(3):
                    r, s = p + a, q + b
                    for c in range(maps):
                        table[tap, s * 4 * maps + r * maps + c, 3 * maps * a + maps * b + c] = 1
                    for k in range(dies):
                        row = 16 * maps + s * 4 * dies + ROW_ORDER.index(r) * dies + k
                        table[tap, row, 3 * maps * a + maps * b + 2 * k] = 1
    return table


def head_selectors(dies):
    table = np.zeros((4, 4 * dies, dies), np.float32)
    for p in range(2):
        for q in range(2):
            for k in range(dies):
                table[2 * p + q, q * 2 * dies + p * dies + k, k] = 1
    return table


def body(
    rows,
    cols,
    dies,
    maps,
    place_ref,
    x_ref,
    xh_ref,
    c_ref,
    ch_ref,
    w1_ref,
    hb_ref,
    dw_ref,
    down_t_ref,
    down_ref,
    mix_t_ref,
    mix_ref,
    up_t_ref,
    up_ref,
    cong_ref,
    bins_ref,
    sel_scr,
    spread_scr,
    mask_scr,
    p_scr,
    feat_scr,
    cpre_scr,
    coarse_scr,
    mixed_scr,
    gskip_scr,
    gmix_scr,
    back_scr,
    cong_scr,
    tap_scr,
    z_scr,
):
    wide = cols + 2 * MARGIN
    span = CHUNK * wide
    lanes = x_ref.shape[1] + xh_ref.shape[1]
    blocks = mix_ref.shape[0] // 128
    width = 2 * cols
    n_full = (rows + 2 * REACH) // CHUNK
    n_mid = (rows + 2 * MIDDLE) // CHUNK
    n_edge = (rows + 2 * EDGE) // CHUNK

    j = lax.broadcasted_iota(jnp.int32, (wide, lanes), 0)
    at = lax.broadcasted_iota(jnp.int32, (wide, lanes), 1)
    want = 2 * (j - MARGIN)
    want = jnp.where(want < 0, want + lanes, want)
    sel_scr[...] = jnp.where(at == want, 1.0, 0.0).astype(bf16)
    j = lax.broadcasted_iota(jnp.int32, (wide, width), 0)
    at = lax.broadcasted_iota(jnp.int32, (wide, width), 1)
    for s in range(4):
        spread_scr[s] = jnp.where(at == 2 * (j - MARGIN) - 1 + s, 1.0, 0.0).astype(bf16)
    column = lax.broadcasted_iota(jnp.int32, (wide, 128), 0) + place_ref[1] - MARGIN
    mask_scr[...] = jnp.where((column >= 0) & (column < place_ref[3]), 1.0, 0.0)
    for scr in (coarse_scr, gmix_scr):
        zero = jnp.zeros((blocks, scr.shape[1], GUARD, 128), f32)
        scr[:, :, 0:GUARD, :] = zero
        scr[:, :, GUARD + wide : 2 * GUARD + wide, :] = zero

    def row_valid(row):
        where = place_ref[0] + row
        inside = (where >= 0) & (where < place_ref[2])
        return jnp.where(inside, 1.0, 0.0).astype(f32)

    def patch_row(ii, carry):
        start = pl.multiple_of(16 * ii + 8, 8)
        part = jnp.concatenate(
            [x_ref[pl.ds(start, 4 * maps), :], xh_ref[pl.ds(start, 4 * maps), :]], axis=1
        )
        shifted = [part if s == 1 else pltpu.roll(part, (1 - s) % lanes, 1) for s in range(4)]
        stacked = jnp.concatenate(shifted, axis=0).astype(bf16)
        p_scr[pl.ds(pl.multiple_of(ii * wide, 16), wide), :] = dot_nt(
            sel_scr[...], stacked
        ).astype(bf16)
        return carry

    lax.fori_loop(0, rows + 2 * REACH, patch_row, 0)

    def first(ch, carry):
        base = pl.multiple_of(ch * span, 16)
        patches = p_scr[pl.ds(base, span), :]
        total = None
        for tap in range(4):
            pre = dot(patches, w1_ref[tap, 0 : 16 * maps, :])
            feat = (pre * sigmoid(pre)).astype(bf16)
            feat_scr[pl.ds(base, span), tap * 256 : (tap + 1) * 256] = feat
            term = dot(feat, down_t_ref[tap])
            total = term if total is None else total + term
        cpre_scr[pl.ds(base, span), :] = total
        coarse = (total * sigmoid(total)).astype(bf16).astype(f32)
        for r in range(CHUNK):
            row = ch * CHUNK + r
            mask = mask_scr[...] * row_valid(row - REACH)
            for b in range(blocks):
                coarse_scr[b, row, GUARD : GUARD + wide, :] = (
                    coarse[r * wide : (r + 1) * wide, b * 128 : (b + 1) * 128] * mask
                )
        return carry

    lax.fori_loop(0, n_full, first, 0)

    def depthwise(src, dst, ch, flipped):
        for b in range(blocks):

            def columns(cb, carry):
                start = cb * 16
                total = [[None, None] for _ in range(CHUNK)]
                for q in range(7):
                    for ri in range(CHUNK + 6):
                        for h in range(2):
                            at = start + (8 * h + q + GUARD - 3)
                            piece = src[b, ch * CHUNK + ri, pl.ds(at, 8), :]
                            for r in range(CHUNK):
                                p = ri - r
                                if 0 <= p < 7:
                                    tap = 7 * p + q
                                    weight = dw_ref[b, 48 - tap if flipped else tap]
                                    term = weight * piece
                                    old = total[r][h]
                                    total[r][h] = term if old is None else old + term
                for r in range(CHUNK):
                    where = pl.multiple_of(r * wide + start, 16)
                    dst[pl.ds(where, 16), b * 128 : (b + 1) * 128] = jnp.concatenate(
                        total[r], axis=0
                    ).astype(bf16)
                return carry

            lax.fori_loop(0, wide // 16, columns, 0)

    def middle(ch, carry):
        depthwise(coarse_scr, mixed_scr, ch, False)
        hidden_pre = dot(mixed_scr[...], mix_t_ref[...])
        s = sigmoid(hidden_pre)
        hidden = hidden_pre * s
        slope_hidden = s + hidden * (1.0 - s)
        hidden = hidden.astype(bf16)
        cot = []
        for r in range(CHUNK):
            at = pl.multiple_of((ch * CHUNK + r) * 2 * dies, 8)
            part = jnp.concatenate(
                [c_ref[pl.ds(at, 2 * dies), :], ch_ref[pl.ds(at, 2 * dies), :]], axis=1
            )
            part = jnp.concatenate([part, pltpu.roll(part, lanes - 1, 1)], axis=0).astype(bf16)
            cot.append(dot_nt(sel_scr[...], part).astype(bf16))
        cot = jnp.concatenate(cot, axis=0)
        base = pl.multiple_of(ch * span, 16)
        at_feat = pl.multiple_of((ch + (REACH - MIDDLE) // CHUNK) * span, 16)
        grad = None
        congestion = [None] * CHUNK
        for tap in range(4):
            lane = slice(tap * 256, (tap + 1) * 256)
            pre = dot(hidden, up_t_ref[tap]) + feat_scr[pl.ds(at_feat, span), lane].astype(f32)
            s = sigmoid(pre)
            act = pre * s
            slope = s + act * (1.0 - s)
            act = act.astype(bf16)
            for r in range(CHUNK):
                term = dot_nt(hb_ref[tap], act[r * wide : (r + 1) * wide])
                congestion[r] = term if tap == 0 else congestion[r] + term
            gskip = (slope * dot(cot, hb_ref[tap])).astype(bf16)
            gskip_scr[pl.ds(base, span), lane] = gskip
            term = dot(gskip, up_ref[tap])
            grad = term if grad is None else grad + term
        for r in range(CHUNK):
            at = pl.multiple_of((ch * CHUNK + r) * 2 * dies, 8)
            for q in range(2):
                cong_scr[q, pl.ds(at, 2 * dies), 0:wide] = congestion[r][
                    q * 2 * dies : (q + 1) * 2 * dies
                ]
        ghidden = (slope_hidden * grad).astype(bf16)
        gmix = dot(ghidden, mix_ref[...]).astype(bf16).astype(f32)
        for r in range(CHUNK):
            for b in range(blocks):
                gmix_scr[b, ch * CHUNK + r, GUARD : GUARD + wide, :] = gmix[
                    r * wide : (r + 1) * wide, b * 128 : (b + 1) * 128
                ]
        return carry

    lax.fori_loop(0, n_mid, middle, 0)

    def last(ch, carry):
        depthwise(gmix_scr, back_scr, ch, True)
        base = pl.multiple_of((ch + (REACH - EDGE) // CHUNK) * span, 16)
        at_skip = pl.multiple_of((ch + (MIDDLE - EDGE) // CHUNK) * span, 16)
        pre = cpre_scr[pl.ds(base, span), :]
        s = sigmoid(pre)
        slope = s + pre * s * (1.0 - s)
        grad = slope * back_scr[...].astype(f32)
        masked = []
        for r in range(CHUNK):
            mask = mask_scr[...] * row_valid(ch * CHUNK + r - EDGE)
            mask = jnp.concatenate([mask] * blocks, axis=1)
            masked.append((grad[r * wide : (r + 1) * wide] * mask).astype(bf16))
        grad = jnp.concatenate(masked, axis=0)
        patches = p_scr[pl.ds(base, span), :]
        taps = [None] * CHUNK
        for tap in range(4):
            lane = slice(tap * 256, (tap + 1) * 256)
            pre = dot(patches, w1_ref[tap, 0 : 16 * maps, :])
            s = sigmoid(pre)
            slope = s + pre * s * (1.0 - s)
            total = gskip_scr[pl.ds(at_skip, span), lane].astype(f32) + dot(grad, down_ref[tap])
            gfeat = (slope * total).astype(bf16)
            weight = w1_ref[tap, 16 * maps : 16 * maps + 16 * dies, :]
            for r in range(CHUNK):
                term = dot_nt(weight, gfeat[r * wide : (r + 1) * wide])
                taps[r] = term if tap == 0 else taps[r] + term
        for r in range(CHUNK):
            high = taps[r].astype(bf16)
            low = (taps[r] - high.astype(f32)).astype(bf16)
            at = pl.multiple_of((ch * CHUNK + r) * 8 * dies, 16)
            for s in range(4):
                piece = slice(s * 4 * dies, (s + 1) * 4 * dies)
                tap_scr[s, pl.ds(at, 4 * dies), 0:wide] = high[piece]
                tap_scr[s, pl.ds(at + 4 * dies, 4 * dies), 0:wide] = low[piece]
        return carry

    lax.fori_loop(0, n_edge, last, 0)

    own = slice(MIDDLE * 2 * dies, (MIDDLE + rows) * 2 * dies)
    cong_ref[...] = (
        dot(cong_scr[0, own, 0:wide].astype(bf16), spread_scr[1])
        + dot(cong_scr[1, own, 0:wide].astype(bf16), spread_scr[2])
    ).astype(bf16)
    z = None
    for s in range(4):
        term = dot(tap_scr[s, :, 0:wide], spread_scr[s])
        z = term if z is None else z + term
    z_scr[...] = z
    lower = lax.broadcasted_iota(jnp.int32, (2 * dies, width), 0) < dies
    step, half = (8 * dies, 4 * dies)

    def rim(i, first_row):
        at = i * step + first_row
        return z_scr[at : at + 2 * dies, :] + z_scr[at + half : at + half + 2 * dies, :]

    for i in range(rows):
        row = rim(i + EDGE, 0) + jnp.where(
            lower, rim(i + EDGE - 1, 2 * dies), rim(i + EDGE + 1, 2 * dies)
        )
        for h in range(width // 128):
            bins_ref[h, i * 2 * dies : (i + 1) * 2 * dies, :] = row[:, h * 128 : (h + 1) * 128]


def network(place, x, xh, c, ch, w1, hb, dw, down_t, down, mix_t, mix, up_t, up, rows, cols):
    dies, maps = (hb.shape[1] // 4, 8)
    wide = cols + 2 * MARGIN
    span = CHUNK * wide
    full, mid, edge = (rows + 2 * REACH, rows + 2 * MIDDLE, rows + 2 * EDGE)
    lanes = x.shape[1] + xh.shape[1]
    channels = mix.shape[0]
    blocks = channels // 128
    guarded = wide + 2 * GUARD
    vmem = pl.BlockSpec(memory_space=pltpu.VMEM)
    return pl.pallas_call(
        functools.partial(body, rows, cols, dies, maps),
        out_shape=(
            jax.ShapeDtypeStruct((rows * 2 * dies, 2 * cols), bf16),
            jax.ShapeDtypeStruct((2 * cols // 128, rows * 2 * dies, 128), f32),
        ),
        in_specs=[pl.BlockSpec(memory_space=pltpu.SMEM)] + [vmem] * 13,
        out_specs=(vmem, vmem),
        scratch_shapes=[
            pltpu.VMEM((wide, lanes), bf16),
            pltpu.VMEM((4, wide, 2 * cols), bf16),
            pltpu.VMEM((wide, 128), f32),
            pltpu.VMEM((full * wide, 16 * maps), bf16),
            pltpu.VMEM((full * wide, 1024), bf16),
            pltpu.VMEM((full * wide, channels), f32),
            pltpu.VMEM((blocks, full, guarded, 128), f32),
            pltpu.VMEM((span, channels), bf16),
            pltpu.VMEM((mid * wide, 1024), bf16),
            pltpu.VMEM((blocks, mid, guarded, 128), f32),
            pltpu.VMEM((span, channels), bf16),
            pltpu.VMEM((2, mid * 2 * dies, 256), f32),
            pltpu.VMEM((4, edge * 8 * dies, 256), bf16),
            pltpu.VMEM((edge * 8 * dies, 2 * cols), f32),
        ],
        compiler_params=pltpu.CompilerParams(vmem_limit_bytes=63_000_000),
        name="network",
    )(place, x, xh, c, ch, w1, hb, dw, down_t, down, mix_t, mix, up_t, up)


def shift(values, axis, forward):
    size = lax.axis_size(axis)
    pairs = [(i, i + 1) if forward else (i + 1, i) for i in range(size - 1)]
    return lax.ppermute(values, axis, pairs)


def local(
    density,
    stem_weight,
    down_weight,
    depth_kernel,
    mix_weight,
    up_weight,
    head_weight,
    cotangent,
    send_blocks,
    cell_slot,
    cell_offset,
    cell_area,
):
    maps, tile_rows, tile_cols = density.shape
    dies, wide = head_weight.shape
    rows, cols = (tile_rows // 2, tile_cols // 2)
    channels = mix_weight.shape[0]
    blocks = channels // 128
    dens = jnp.transpose(density, (1, 0, 2))
    cot = jnp.transpose(cotangent, (1, 0, 2)).reshape(rows, 2 * dies, tile_cols)
    deep, shallow = (2 * (REACH + 1), MIDDLE)
    last = jnp.concatenate([dens[-deep:], cot[-shallow:]], axis=0)
    first = jnp.concatenate([dens[:deep], cot[:shallow]], axis=0)
    above = shift(last, "ty", True)
    below = shift(first, "ty", False)
    main = jnp.concatenate(
        [above[:deep], dens, below[:deep], above[deep:], cot, below[deep:]], axis=0
    )
    side = 2 * MARGIN
    left = shift(main[:, :, -side:], "tx", True)
    right = shift(main[:, :, :side], "tx", False)
    gap = jnp.zeros(main.shape[:2] + (128 - 2 * side,), main.dtype)
    rim = jnp.concatenate([right, gap, left], axis=2)
    deep_rows = tile_rows + 2 * deep
    main = main.astype(f32)
    rim = rim.astype(f32)
    x = main[:deep_rows].reshape(-1, tile_cols)
    xh = rim[:deep_rows].reshape(-1, 128)
    c = main[deep_rows:].reshape(-1, tile_cols)
    ch = rim[deep_rows:].reshape(-1, 128)
    stem_table = jnp.asarray(stem_selectors(maps, dies), bf16)
    w1 = jnp.einsum("tsk,ok->tso", stem_table, stem_weight, preferred_element_type=f32).astype(
        bf16
    )
    head_table = jnp.asarray(head_selectors(dies), bf16)
    hb = jnp.einsum("tsk,ko->tso", head_table, head_weight, preferred_element_type=f32).astype(
        bf16
    )
    dw = depth_kernel.reshape(blocks, 128, 49).transpose(0, 2, 1)
    center = (jnp.arange(49) == 24).astype(f32)
    dw = jnp.broadcast_to((dw + center[None, :, None])[:, :, None, :], (blocks, 49, 8, 128))
    place = jnp.stack(
        [
            lax.axis_index("ty") * rows,
            lax.axis_index("tx") * cols,
            lax.axis_size("ty") * rows,
            lax.axis_size("tx") * cols,
        ]
    ).astype(jnp.int32)
    cong, bins = network(
        place,
        x,
        xh,
        c,
        ch,
        w1,
        hb,
        dw,
        jnp.swapaxes(down_weight, 1, 2),
        down_weight,
        mix_weight.T,
        mix_weight,
        jnp.swapaxes(up_weight, 1, 2),
        up_weight,
        rows,
        cols,
    )
    congestion = jnp.transpose(cong.reshape(tile_rows, dies, tile_cols), (1, 0, 2))
    halves = tile_cols // 128
    per_die = tile_rows * halves
    block = send_blocks[0]
    die, inside = (block // per_die, block % per_die)
    where = (inside % halves) * (tile_rows * dies) + (inside // halves) * dies + die
    outgoing = bins.reshape(-1, 128).at[where].get(mode="promise_in_bounds")
    received = lax.all_to_all(outgoing, ("ty", "tx"), split_axis=0, concat_axis=0, tiled=True)
    slot_count = received.shape[0]
    slot_hot = (cell_slot[:, None] == jnp.arange(slot_count, dtype=jnp.int32)[None, :]).astype(f32)
    block_rows = jnp.dot(slot_hot, received, precision=lax.Precision.HIGHEST)
    offset_hot = (cell_offset[:, None] == jnp.arange(128, dtype=jnp.int32)[None, :]).astype(f32)
    cell_grad = cell_area * jnp.sum(block_rows * offset_hot, axis=1)
    return (congestion, cell_grad)


def solution(mesh):
    in_specs = (
        P(None, "ty", "tx"),
        P(),
        P(),
        P(),
        P(),
        P(),
        P(),
        P(None, "ty", "tx"),
        P(("ty", "tx"), None),
        P(("ty", "tx")),
        P(("ty", "tx")),
        P(("ty", "tx")),
    )
    out_specs = (P(None, "ty", "tx"), P(("ty", "tx")))
    return jax.shard_map(local, mesh=mesh, in_specs=in_specs, out_specs=out_specs, check_vma=False)
```

time: 923 us -> 153 us (0.17); the launches traced: 913 us -> 153 us
  other arithmetic: 279 us -> 1.52 us
  local copies, waits for them, and re-layouts: 246 us -> 14.6 us
  blocking collectives: 212 us -> 0 us
  Pallas kernels: 0 us -> 108 us
  waiting for transfers between devices: 80.2 us -> 7.49 us
  matrix products: 51.3 us -> 3.07 us
  starting transfers between devices: 42.4 us -> 16.7 us
    broadcast_in_dim x2 -> x0, other arithmetic: 215 us -> none  [depth_block(): result[None]]
    all_to_all x4 -> x0, blocking collectives: 212 us -> none  [the longest x2 108 us: depth_block(): lax.all_to_all(feature_map, 'ty', split_axis=0, concat_axis=1, tiled=True)]
    pallas_call x0 -> x1, Pallas kernels: none -> 108 us  [network(): pl.pallas_call(functools.partial(body, rows, cols, dies, maps), out_shape...]
    all_to_all x9 -> x0, local copies, waits for them, and re-layouts: 91.5 us -> none  [the longest x2 48.9 us: depth_block(): lax.all_to_all(result[None], 'ty', split_axis=2, concat_axis=0, tiled=True)]
    unnamed x52 -> x33, local copies, waits for them, and re-layouts: 79.2 us -> 5.94 us
    all_to_all x4 -> x0, waiting for transfers between devices: 71.5 us -> none  [the longest x2 50.7 us: depth_block(): lax.all_to_all(lax.all_to_all(feature_map, 'ty', split_axis=0, concat_axi...]
    dot_general x25 -> x2, matrix products: 50.1 us -> 1.84 us  [the longest x1 1.05 us: local(): jnp.einsum('tsk,ok->tso', stem_table, stem_weight, preferred_element_type...]
    convert_element_type x6 -> x2, other arithmetic: 42.5 us -> 0.13 us  [the longest x1 0.12 us: local(): rim = rim.astype(f32)]
  transfers between devices with their start and end apart: 13 -> 5, of which waited for: 6 -> 2; matrix products, arithmetic and copies ran while one was open for 5% -> 6% of each run, Pallas kernels for 0% -> 0%
where the time goes in v1:
time: 153 us
  Pallas kernels  108 us (71%)
  starting transfers between devices  16.7 us (11%)
  local copies, waits for them, and re-layouts  14.6 us (10%)
  waiting for transfers between devices  7.49 us (5%)
  matrix products  3.07 us (2%)
    pallas_call x1, Pallas kernels, network(): pl.pallas_call(functools.partial(body, rows, cols, dies, maps), out_shape...  108 us
    ppermute x4, starting transfers between devices, shift(): return lax.ppermute(values, axis, pairs)  10.5 us
    all_to_all x1, waiting for transfers between devices, local(): lax.all_to_all(outgoing, ('ty', 'tx'), split_axis=0, concat_axis=0, tiled...  6.71 us
    all_to_all x1, starting transfers between devices, local(): lax.all_to_all(outgoing, ('ty', 'tx'), split_axis=0, concat_axis=0, tiled...  6.17 us
    unnamed x33, local copies, waits for them, and re-layouts  5.94 us
  transfers between devices with their start and end apart: 5, of which 2 were waited for; matrix products, arithmetic and copies ran while one was open for 6% of the time, Pallas kernels for 0%

profile of v1, /device:TPU:0, one launch (start us, length us, event | category | flops | bytes accessed | tf_op | source)
XLA Modules:
  0.0 152.8 jit_solution(13140057573339961159)
XLA Ops:
  0.6 0.0 copy-start
  0.6 0.0 copy-start.6
  0.7 0.9 fusion.10
  1.6 0.0 copy-done.6
  1.7 4.9 %collective-permute-start = (bf16[20,8,256]{2,0,1:T(8,128)(2,1)S(1)}, bf16[20,8,256]{2,0,1:T(8,128)(2,1)S(1)}, u32[]{:S(2)}, u32[]{:S(2)}) collective-permute-start(bf16[20,8,256]{2,0,1:T(8,128)(2,1)S(1)} %pad_maximum_fusion), channel_id=1, source_target_pairs={{0,4},{4,8},{8,12},{12,16},{16,20},{20,24},{24,28},{1,5},{5,9},{9,... | collective-permute-start | bytes 245768 | tf_op jit(solution)/shard_map/ppermute | solution.py:350
  6.6 1.3 collective-permute-start.1
  7.9 0.1 copy.29
  8.0 0.0 copy-start.7
  8.1 0.8 copy-done.7
  8.9 0.0 copy-start.14
  9.0 0.6 copy-done.14
  9.6 0.0 copy-start.5
  9.6 0.1 fusion.2
  9.7 0.0 copy-done
  9.7 0.8 copy-done.5
  10.5 0.0 copy-start.10
  10.5 0.0 copy-start.11
  10.5 0.0 copy-start.4
  10.5 1.0 convolution_convert_fusion.w1_ref
  11.5 0.0 copy-done.10
  11.6 0.0 copy-done.11
  11.6 0.0 copy-start.1
  11.6 0.8 convolution_convert_fusion.1.hb_ref
  12.4 0.0 collective-permute-done
  12.4 0.8 collective-permute-done.1
  13.2 0.0 copy-done.4
  13.2 0.3 concatenate.14
  13.5 0.1 fusion.9
  13.6 1.3 collective-permute-start.2
  14.9 3.0 %collective-permute-start.3 = (bf16[88,8,16]{2,0,1:T(8,128)(2,1)S(1)}, bf16[88,8,16]{2,0,1:T(8,128)(2,1)S(1)}, u32[]{:S(2)}, u32[]{:S(2)}) collective-permute-start(bf16[88,8,16]{2,0,1:T(8,128)(2,1)S(1)} %get-tuple-element.7), channel_id=1, source_target_pairs={{0,1},{1,2},{2,3},{4,5},{5,6},{6,7},{8,9},{9,10},{10,11},{12,13},{... | collective-permute-start | bytes 67592 | tf_op jit(solution)/shard_map/ppermute | solution.py:350
  17.9 0.7 pad_add_fusion.place_ref
  18.6 0.0 copy-done.1
  18.6 0.0 copy-start.2
  18.6 1.3 copy.36
  19.9 0.0 copy-done.2
  19.9 0.0 copy-start.3
  19.9 1.3 copy.38
  21.2 0.0 copy-done.3
  21.2 1.0 copy.37
  22.2 0.1 pad.1.clone
  22.4 1.1 copy.46
  23.5 0.7 copy.47
  24.2 0.0 collective-permute-done.2
  24.3 0.0 collective-permute-done.3
  24.3 0.1 maximum_convert_fusion
  24.4 0.7 slice_bitcast_fusion.xh_ref
  25.1 0.6 slice_bitcast_fusion.1.ch_ref
  25.8 0.9 broadcast_in_dim.5.dw_ref
  26.7 108.5 %network.1 = (bf16[128,256]{1,0:T(8,128)(2,1)}, f32[2,128,128]{2,1,0:T(8,128)}) custom-call(s32[4]{0:T(128)} %pad_add_fusion.place_ref, f32[512,256]{1,0:T(8,128)} %bitcast.56, f32[512,128]{1,0:T(8,128)} %slice_bitcast_fusion.xh_ref, f32[192,256]{1,0:T(8,128)} %bitcast.58, f32[192,128]{1,0:T(8,128)} %slice_bitcast_fusion.1.ch_ref, ...), custom_call_target="tpu_custom_call" | custom-call | tf_op jit(solution)/shard_map/network/pallas_call | solution.py:318
  135.2 2.1 %gather_fusion = f32[128,128]{1,0:T(8,128)} fusion(f32[256,128]{1,0:T(8,128)} %bitcast.57, s32[1024]{0:T(1024)S(1)} %pad_clamp_fusion), kind=kCustom, calls=%fused_computation | custom fusion | bytes 131584 | tf_op jit(solution)/shard_map/gather | solution.py:437
  137.3 0.0 copy-start.8
  137.3 6.2 %all-to-all-start = ((f32[32,4,128]{2,1,0:T(4,128)}), f32[32,4,128]{2,1,0:T(4,128)S(1)}, u32[]{:S(2)}, u32[]{:S(2)}) async-start(f32[32,4,128]{2,1,0:T(4,128)} %bitcast.18), calls=%async_computation | async-start | bytes 131072 | tf_op jit(solution)/shard_map/all_to_all | solution.py:438
  143.5 0.0 copy-done.8
  143.5 0.0 copy-start.12
  143.5 0.0 copy-start.13
  143.6 0.6 copy.48
  144.2 6.7 %all-to-all-done = f32[32,4,128]{2,1,0:T(4,128)S(1)} async-done(((f32[32,4,128]{2,1,0:T(4,128)}), f32[32,4,128]{2,1,0:T(4,128)S(1)}, u32[]{:S(2)}, u32[]{:S(2)}) %all-to-all-start) | async-done | bytes 65568 | tf_op jit(solution)/shard_map/all_to_all | solution.py:438
  150.9 0.0 copy-done.12
  150.9 0.0 copy-done.13
  150.9 0.0 copy-start.9
  150.9 1.2 fusion
  152.2 0.0 copy-done.9
  152.2 0.6 mul.45
  (25 shorter events, 0.3 us)
Async XLA Ops:
  0.6 9.1 %copy-start = (bf16[256,72]{0,1:T(8,128)(2,1)S(1)}, bf16[256,72]{0,1:T(8,128)(2,1)}, u32[]{:S(2)}) copy-start(bf16[256,72]{0,1:T(8,128)(2,1)} %param.15) | copy-start | bytes 110596
  0.6 0.9 copy-start.6
  1.7 10.7 %collective-permute-start = (bf16[20,8,256]{2,0,1:T(8,128)(2,1)S(1)}, bf16[20,8,256]{2,0,1:T(8,128)(2,1)S(1)}, u32[]{:S(2)}, u32[]{:S(2)}) collective-permute-start(bf16[20,8,256]{2,0,1:T(8,128)(2,1)S(1)} %pad_maximum_fusion), channel_id=1, source_target_pairs={{0,4},{4,8},{8,12},{12,16},{16,20},{20,24},{24,28},{1,5},{5,9},{9,... | collective-permute-start | bytes 245768 | tf_op jit(solution)/shard_map/ppermute | solution.py:350
  6.6 6.5 %collective-permute-start.1 = (bf16[20,8,256]{2,0,1:T(8,128)(2,1)S(1)}, bf16[20,8,256]{2,0,1:T(8,128)(2,1)S(1)}, u32[]{:S(2)}, u32[]{:S(2)}) collective-permute-start(bf16[20,8,256]{2,0,1:T(8,128)(2,1)S(1)} %pad_maximum_fusion.1), channel_id=1, source_target_pairs={{4,0},{8,4},{12,8},{16,12},{20,16},{24,20},{28,24},{5,1},{9,5},{13... | collective-permute-start | bytes 245768 | tf_op jit(solution)/shard_map/ppermute | solution.py:350
  8.0 0.9 copy-start.7
  8.9 0.7 copy-start.14
  9.6 0.9 copy-start.5
  10.5 1.1 copy-start.10
  10.5 1.1 copy-start.11
  10.5 2.7 %copy-start.4 = (bf16[8,32,256]{2,1,0:T(8,128)(2,1)S(1)}, bf16[8,32,256]{2,1,0:T(8,128)(2,1)}, u32[]{:S(2)}) copy-start(bf16[8,32,256]{2,1,0:T(8,128)(2,1)} %param.14) | copy-start | bytes 393220
  11.6 7.0 %copy-start.1 = (bf16[4,512,256]{2,1,0:T(8,128)(2,1)S(1)}, bf16[4,512,256]{2,1,0:T(8,128)(2,1)}, u32[]{:S(2)}) copy-start(bf16[4,512,256]{2,1,0:T(8,128)(2,1)} %down_ref.1) | copy-start | bytes 3145732
  13.6 10.6 %collective-permute-start.2 = (bf16[88,8,16]{2,0,1:T(8,128)(2,1)S(1)}, bf16[88,8,16]{2,0,1:T(8,128)(2,1)S(1)}, u32[]{:S(2)}, u32[]{:S(2)}) collective-permute-start(bf16[88,8,16]{2,0,1:T(8,128)(2,1)S(1)} %get-tuple-element.6), channel_id=1, source_target_pairs={{1,0},{2,1},{3,2},{5,4},{6,5},{7,6},{9,8},{10,9},{11,10},{13,12},{... | collective-permute-start | bytes 67592 | tf_op jit(solution)/shard_map/ppermute | solution.py:350
  14.9 9.4 %collective-permute-start.3 = (bf16[88,8,16]{2,0,1:T(8,128)(2,1)S(1)}, bf16[88,8,16]{2,0,1:T(8,128)(2,1)S(1)}, u32[]{:S(2)}, u32[]{:S(2)}) collective-permute-start(bf16[88,8,16]{2,0,1:T(8,128)(2,1)S(1)} %get-tuple-element.7), channel_id=1, source_target_pairs={{0,1},{1,2},{2,3},{4,5},{5,6},{6,7},{8,9},{9,10},{10,11},{12,13},{... | collective-permute-start | bytes 67592 | tf_op jit(solution)/shard_map/ppermute | solution.py:350
  18.6 1.3 copy-start.2
  19.9 1.3 copy-start.3
  137.3 6.2 %copy-start.8 = (bf16[128,256]{1,0:T(8,128)(2,1)S(1)}, bf16[128,256]{1,0:T(8,128)(2,1)}, u32[]{:S(2)}) copy-start(bf16[128,256]{1,0:T(8,128)(2,1)} %get-tuple-element.4) | copy-start | bytes 196612
  137.3 13.6 %all-to-all-start = ((f32[32,4,128]{2,1,0:T(4,128)}), f32[32,4,128]{2,1,0:T(4,128)S(1)}, u32[]{:S(2)}, u32[]{:S(2)}) async-start(f32[32,4,128]{2,1,0:T(4,128)} %bitcast.18), calls=%async_computation | async-start | bytes 131072 | tf_op jit(solution)/shard_map/all_to_all | solution.py:438
  143.5 7.4 %copy-start.12 = (s32[2048]{0:T(1024)S(1)}, s32[2048]{0:T(1024)}, u32[]{:S(2)}) copy-start(s32[2048]{0:T(1024)} %param.23) | copy-start | bytes 24580
  143.5 7.4 %copy-start.13 = (s32[2048]{0:T(1024)S(1)}, s32[2048]{0:T(1024)}, u32[]{:S(2)}) copy-start(s32[2048]{0:T(1024)} %param.24) | copy-start | bytes 24580
  150.9 1.2 copy-start.9
